TPU v7x, 128 devices: a whole 4x4x4 slice. The times are simulated.
128 devices in a mesh: occ: 4 (over x), vir: 32 (over y, z, core).
Axes of the slice: x: 4, y: 4, z: 4, core: 2. Of those that a mesh axis runs over, the one named last changes fastest.
Arguments:
- amplitudes: bfloat16 [256, 262144], P('occ', 'vir'), may hold values from -6 to 6
- cycle_integrals: bfloat16 [16, 64, 16, 64], P(None, None, 'occ'), may hold values from -0.1875 to 0.1875
- ladder_tiles: bfloat16 [2048, 4, 128, 128], P('vir'), may hold values from -0.25 to 0.25
- ladder_rows: int32 [2048, 4], P('vir'), may hold values from 0 to 2047, as said below
- ladder_count: int32 [2048], P('vir'), may hold values from 2 to 4
- row_gap: float32 [256], P('occ'), may hold values from 1 to 3
- column_energy: float32 [262144], P('vir'), may hold values from 0.5 to 8
Outputs:
- updated: bfloat16 [256, 262144], P('occ', 'vir')
Inputs may be any that keep to these rules, and one draw needn't show every extreme that they name: `ladder_rows`: each entry of column tile c's list names a virtual-pair tile within 2 tiles of c; entry 0 is max(c - 2, 0) and entry 1 is min(c + 2, 2047).
All inputs are finite; a program needn't handle non-finite values.
Results may differ from a plain program's by a relative error of at most 0.0019.
Values may be sent and summed in bfloat16 or wider, within the bound.
A program may use at most 192 MiB of HBM per device.

v0:
```python
import jax
import jax.numpy as jnp
from jax import lax
from jax.sharding import PartitionSpec as P

TILE = 128
NJ = 16
NA = 4096
NB_DEV = 2
KMAX = 4
HT = 2


def extended(block, sides, width):
    for axis, dim in sides:
        count = lax.axis_size(axis)
        forward = [(i, i + 1) for i in range(count - 1)]
        backward = [(target, source) for source, target in forward]
        low = lax.ppermute(
            lax.slice_in_dim(block, block.shape[dim] - width, None, axis=dim), axis, forward
        )
        high = lax.ppermute(lax.slice_in_dim(block, 0, width, axis=dim), axis, backward)
        block = jnp.concatenate([low, block, high], axis=dim)
    return block


def local(
    amplitudes, cycle_integrals, ladder_tiles, ladder_rows, ladder_count, row_gap, column_energy
):
    rows_dev = amplitudes.shape[0]
    cols_dev = amplitudes.shape[1]
    outer_occ = rows_dev // NJ
    four_dim = amplitudes.reshape(outer_occ, NJ, NB_DEV, NA)
    cycle_input = lax.all_to_all(four_dim, "vir", split_axis=3, concat_axis=2, tiled=True)
    tiles_dev = cols_dev // TILE
    padded = extended(amplitudes, (("vir", 1),), HT * TILE)
    own_tiles = lax.axis_index("vir") * tiles_dev + jnp.arange(tiles_dev, dtype=jnp.int32)
    relative = ladder_rows - own_tiles[:, None]
    live_mask = jnp.arange(KMAX, dtype=jnp.int32)[None, :] < ladder_count[:, None]
    ladder = jnp.zeros((rows_dev, tiles_dev, TILE), jnp.float32)
    for offset in range(2 * HT + 1):
        window = padded[:, offset * TILE : offset * TILE + cols_dev].reshape(
            rows_dev, tiles_dev, TILE
        )
        for entry in range(KMAX):
            selected = live_mask[:, entry] & (relative[:, entry] == offset - HT)
            masked = jnp.where(
                selected[:, None, None], ladder_tiles[:, entry], jnp.zeros((), jnp.bfloat16)
            )
            ladder = ladder + jnp.einsum(
                "rcp,cpq->rcq", window, masked, preferred_element_type=jnp.float32
            )
    ladder = ladder.reshape(rows_dev, cols_dev)
    all_rows = lax.all_gather(cycle_input, "occ", axis=0, tiled=True)
    cycle_part = jnp.einsum(
        "ijba,jbkc->ikca", all_rows, cycle_integrals, preferred_element_type=jnp.float32
    ).astype(jnp.bfloat16)
    cycle_pair = lax.all_to_all(
        lax.all_to_all(cycle_part, "occ", split_axis=0, concat_axis=1, tiled=True),
        "vir",
        split_axis=2,
        concat_axis=3,
        tiled=True,
    )
    cycle_flat = cycle_pair.reshape(rows_dev, cols_dev)
    denominator = row_gap[:, None] + column_energy[None, :]
    updated = (
        amplitudes.astype(jnp.float32) + (cycle_flat.astype(jnp.float32) + ladder) / denominator
    )
    return updated.astype(jnp.bfloat16)


def solution(mesh):
    in_specs = (
        P("occ", "vir"),
        P(None, None, "occ", None),
        P("vir", None, None, None),
        P("vir", None),
        P("vir"),
        P("occ"),
        P("vir"),
    )
    out_specs = P("occ", "vir")
    return jax.shard_map(local, mesh=mesh, in_specs=in_specs, out_specs=out_specs, check_vma=False)
```

profile of v0, /device:TPU:1, one launch (start us, length us, event | category | flops | bytes accessed | tf_op | source)
XLA Modules:
  0.0 194.8 jit_solution(11123908715003614297)
XLA Ops:
  7.3 4.9 %collective-permute-start = (bf16[64,256]{1,0:T(8,128)(2,1)S(1)}, bf16[64,256]{1,0:T(8,128)(2,1)S(1)}, u32[]{:S(2)}, u32[]{:S(2)}) collective-permute-start(bf16[64,256]{1,0:T(8,128)(2,1)S(1)} %get-tuple-element.11), channel_id=1, source_target_pairs={{0,1},{1,2},{2,3},{3,4},{4,5},{5,6},{6,7},{7,8},{8,9},{9,10},{10,1... | collective-permute-start | bytes 98312 | tf_op jit(solution)/shard_map/ppermute | solution.py:19
  16.0 9.4 %copy.133 = bf16[4,16,2,4096]{1,0,2,3:T(4,128)(2,1)} copy(bf16[4,16,2,4096]{3,2,1,0:T(2,128)(2,1)S(1)} %reshape.294) | data formatting | bytes 2097152 | tf_op jit(solution)/shard_map/reshape | solution.py:33
  25.5 11.2 %reshape.306 = bf16[32,2,8192]{2,1,0:T(2,128)(2,1)} reshape(bf16[4096,2,4,16]{3,2,1,0:T(4,128)(2,1)} %bitcast.213) | data formatting | bytes 2097152
  36.7 8.4 %all-to-all-start = ((bf16[32,2,8192]{2,1,0:T(2,128)(2,1)}), bf16[32,2,8192]{2,1,0:T(2,128)(2,1)S(1)}, u32[]{:S(2)}, u32[]{:S(2)}) async-start(bf16[32,2,8192]{2,1,0:T(2,128)(2,1)} %reshape.306), calls=%async_computation | async-start | bytes 2097152 | tf_op jit(solution)/shard_map/all_to_all | solution.py:34
  45.3 3.7 %fusion.12 = f32[64,128,64]{1,2,0:T(8,128)} fusion(pred[64]{0:T(512)(128)(4,1)S(1)} %get-tuple-element.23, bf16[64,4,128,128]{3,2,1,0:T(8,128)(2,1)} %param.9, bf16[64,8192]{1,0:T(8,128)(2,1)S(1)} %copy-done), kind=kOutput, calls=%fused_computation.23 | convolution fusion | flops 135266304 | bytes 5242944 | tf_op jit(solution)/shard_map/rcp,cpq->rcq/dot_general | solution.py:50
  49.0 3.6 %fusion.17 = f32[64,128,64]{1,2,0:T(8,128)} fusion(pred[64]{0:T(512)(128)(4,1)S(1)} %get-tuple-element.15, bf16[64,4,128,128]{3,2,1,0:T(8,128)(2,1)} %param.9, bf16[64,8192]{1,0:T(8,128)(2,1)S(1)} %copy-done), kind=kOutput, calls=%fused_computation.33 | convolution fusion | flops 135266304 | bytes 5242944 | tf_op jit(solution)/shard_map/rcp,cpq->rcq/dot_general | solution.py:50
  52.6 3.7 %fusion.23 = f32[64,128,64]{1,2,0:T(8,128)} fusion(pred[64]{0:T(512)(128)(4,1)S(1)} %get-tuple-element.19, bf16[64,4,128,128]{3,2,1,0:T(8,128)(2,1)} %param.9, bf16[64,8192]{1,0:T(8,128)(2,1)S(1)} %copy-done), kind=kOutput, calls=%fused_computation.48 | convolution fusion | flops 135266304 | bytes 5242944 | tf_op jit(solution)/shard_map/rcp,cpq->rcq/dot_general | solution.py:50
  56.3 5.7 %all-to-all-done = bf16[32,2,8192]{2,1,0:T(2,128)(2,1)S(1)} async-done(((bf16[32,2,8192]{2,1,0:T(2,128)(2,1)}), bf16[32,2,8192]{2,1,0:T(2,128)(2,1)S(1)}, u32[]{:S(2)}, u32[]{:S(2)}) %all-to-all-start) | async-done | bytes 1048608 | tf_op jit(solution)/shard_map/all_to_all | solution.py:34
  62.0 7.6 %reshape.307 = bf16[4096,2,4,16]{3,2,1,0:T(4,128)(2,1)} reshape(bf16[32,2,8192]{2,1,0:T(2,128)(2,1)S(1)} %all-to-all-done) | data formatting | bytes 2097152
  69.6 12.8 %copy.134 = bf16[4,16,32,2,128]{4,3,2,1,0:T(2,128)(2,1)} copy(bf16[4,16,32,2,128]{1,0,3,4,2:T(4,128)(2,1)} %bitcast.214) | data formatting | bytes 2097152 | tf_op jit(solution)/shard_map/all_to_all | solution.py:34
  82.4 3.9 %fusion.7 = f32[64,128,64]{1,2,0:T(8,128)} fusion(pred[64]{0:T(512)(128)(4,1)S(1)} %get-tuple-element.27, bf16[64,4,128,128]{3,2,1,0:T(8,128)(2,1)} %param.9, bf16[64,8192]{1,0:T(8,128)(2,1)S(1)} %copy-done), kind=kOutput, calls=%fused_computation.13 | convolution fusion | flops 135266304 | bytes 5242944 | tf_op jit(solution)/shard_map/rcp,cpq->rcq/dot_general | solution.py:50
  87.2 2.2 %slice-done.1 = s8[4194304]{0:T(1024)(128)(4,1)S(1)} async-done(((s8[8388608]{0:T(1024)(128)(4,1)}), s8[4194304]{0:T(1024)(128)(4,1)S(1)}, s32[]{:S(2)}) %slice-start.1) | async-done | bytes 4194328
  114.5 13.6 %all-gather.2.cloned.1.call-done = bf16[16,16,64,128]{3,2,1,0:T(8,128)(2,1)} async-done(((bf16[4,16,64,128]{3,2,1,0:T(8,128)(2,1)}), bf16[16,16,64,128]{3,2,1,0:T(8,128)(2,1)}) %all-gather.2.cloned.1.call-update) | async-done | bytes 4194320 | tf_op jit(solution)/shard_map/all_gather | solution.py:54
  128.1 3.5 %fusion.48 = bf16[16,4,64,128]{3,2,0,1:T(8,128)(2,1)S(1)} fusion(bf16[16,16,64,128]{3,2,1,0:T(8,128)(2,1)} %all-gather.2.cloned.1.call-done, bf16[16,64,4,64,1]{3,2,1,0,4:T(4,128)(2,1)S(1)} %bitcast.221), kind=kOutput, calls=%fused_computation.72 | convolution fusion | flops 1074266112 | bytes 5767168 | tf_op jit(solution)/shard_map/ijba,jbkc->ikca/dot_general | solution.py:55
  132.6 3.7 %all-to-all-start.1 = ((bf16[16,4,64,128]{3,2,1,0:T(8,128)(2,1)}), bf16[16,4,64,128]{3,2,1,0:T(8,128)(2,1)S(1)}, u32[]{:S(2)}, u32[]{:S(2)}) async-start(bf16[16,4,64,128]{3,2,1,0:T(8,128)(2,1)} %copy.136), calls=%async_computation.1 | async-start | bytes 2097152 | tf_op jit(solution)/shard_map/all_to_all | solution.py:59
  136.4 4.0 %fusion.6 = f32[64,128,64]{1,2,0:T(8,128)} fusion(pred[64]{0:T(512)(128)(4,1)S(1)} %get-tuple-element.26, bf16[64,4,128,128]{3,2,1,0:T(8,128)(2,1)} %param.9, bf16[8,64,8,128]{3,2,1,0:T(8,128)(2,1)} %copy-done.2), kind=kOutput, calls=%fused_computation.12 | convolution fusion | flops 135266304 | bytes 5242944 | tf_op jit(solution)/shard_map/rcp,cpq->rcq/dot_general | solution.py:50
  140.4 3.6 %fusion.10 = f32[64,128,64]{1,2,0:T(8,128)} fusion(pred[64]{0:T(512)(128)(4,1)S(1)} %get-tuple-element.32, bf16[64,4,128,128]{3,2,1,0:T(8,128)(2,1)} %param.9, bf16[8,64,8,128]{3,2,1,0:T(8,128)(2,1)S(1)} %get-tuple-element.5), kind=kOutput, calls=%fused_computation.21 | convolution fusion | flops 135266304 | bytes 5242944 | tf_op jit(solution)/shard_map/rcp,cpq->rcq/dot_general | solution.py:50
  144.0 3.6 %fusion.15 = f32[64,128,64]{1,2,0:T(8,128)} fusion(pred[64]{0:T(512)(128)(4,1)S(1)} %get-tuple-element.31, bf16[64,4,128,128]{3,2,1,0:T(8,128)(2,1)} %param.9, bf16[8,64,8,128]{3,2,1,0:T(8,128)(2,1)S(1)} %get-tuple-element.5), kind=kOutput, calls=%fused_computation.31 | convolution fusion | flops 135266304 | bytes 5242944 | tf_op jit(solution)/shard_map/rcp,cpq->rcq/dot_general | solution.py:50
  147.7 2.8 %all-to-all-done.1 = bf16[16,4,64,128]{3,2,1,0:T(8,128)(2,1)S(1)} async-done(((bf16[16,4,64,128]{3,2,1,0:T(8,128)(2,1)}), bf16[16,4,64,128]{3,2,1,0:T(8,128)(2,1)S(1)}, u32[]{:S(2)}, u32[]{:S(2)}) %all-to-all-start.1) | async-done | bytes 1048608 | tf_op jit(solution)/shard_map/all_to_all | solution.py:59
  152.2 8.8 %all-to-all-start.2 = ((bf16[4,16,64,128]{3,1,0,2:T(8,128)(2,1)}), bf16[4,16,64,128]{3,1,0,2:T(8,128)(2,1)}, u32[]{:S(2)}, u32[]{:S(2)}) async-start(bf16[4,16,64,128]{3,1,0,2:T(8,128)(2,1)} %copy.138), calls=%async_computation.2 | async-start | bytes 2097152 | tf_op jit(solution)/shard_map/all_to_all | solution.py:58
  161.0 15.6 %fusion.20 = f32[64,8,8,128]{3,2,1,0:T(8,128)S(1)} fusion(f32[64,128,64]{1,2,0:T(8,128)} %fusion.9, f32[64,128,64]{1,2,0:T(8,128)} %fusion.14, f32[64,128,64]{1,2,0:T(8,128)} %fusion.19, f32[64,128,64]{1,2,0:T(8,128)} %fusion.8, f32[64,128,64]{1,2,0:T(8,128)} %fusion.13, f32[64,128,64]{1,2,0:T(8,128)} %fusion.24, f32[64,128,64]{1,2,0:T(8,128)} %fusion.18, ...), kind=kOutput, calls=%fused_computation.38 | convolution fusion | flops 145227776 | bytes 45088832 | tf_op jit(solution)/shard_map/rcp,cpq->rcq/dot_general | solution.py:50
  179.6 2.6 %copy.140 = f32[4,16,2,32,128]{4,3,2,1,0:T(8,128)} copy(f32[4,16,2,32,128]{4,1,2,3,0:T(8,128)S(1)} %convert_bitcast_fusion) | data formatting | bytes 4194304 | tf_op jit(solution)/shard_map/convert_element_type | solution.py:68
  182.2 2.7 %reshape.301 = f32[64,8192]{1,0:T(8,128)} reshape(f32[4,16,2,32,128]{4,3,2,1,0:T(8,128)} %copy.140) | data formatting | bytes 4194304 | tf_op jit(solution)/shard_map/convert_element_type | solution.py:68
  184.9 3.1 %fusion.4 = bf16[64,8192]{1,0:T(8,128)(2,1)} fusion(f32[64,8192]{1,0:T(8,128)} %reshape.301, f32[64,8,8,128]{3,2,1,0:T(8,128)S(1)} %fusion.20, bf16[64,8192]{1,0:T(8,128)(2,1)S(1)} %copy-done, f32[8192]{0:T(1024)S(1)} %copy-done.3, f32[64]{0:T(128)S(1)} %copy-done.5), kind=kLoop, calls=%fused_computation.5 | loop fusion | flops 3145728 | bytes 6324480 | tf_op jit(solution)/shard_map/convert_element_type | solution.py:70
  (56 shorter events, 36.4 us)
Async XLA Ops:
  7.3 79.0 %collective-permute-start = (bf16[64,256]{1,0:T(8,128)(2,1)S(1)}, bf16[64,256]{1,0:T(8,128)(2,1)S(1)}, u32[]{:S(2)}, u32[]{:S(2)}) collective-permute-start(bf16[64,256]{1,0:T(8,128)(2,1)S(1)} %get-tuple-element.11), channel_id=1, source_target_pairs={{0,1},{1,2},{2,3},{3,4},{4,5},{5,6},{6,7},{7,8},{8,9},{9,10},{10,1... | collective-permute-start | bytes 98312 | tf_op jit(solution)/shard_map/ppermute | solution.py:19
  12.2 74.3 %collective-permute-start.1 = (bf16[64,256]{1,0:T(8,128)(2,1)S(1)}, bf16[64,256]{1,0:T(8,128)(2,1)S(1)}, u32[]{:S(2)}, u32[]{:S(2)}) collective-permute-start(bf16[64,256]{1,0:T(8,128)(2,1)S(1)} %get-tuple-element.12), channel_id=1, source_target_pairs={{1,0},{2,1},{3,2},{4,3},{5,4},{6,5},{7,6},{8,7},{9,8},{10,9},{11,1... | collective-permute-start | bytes 98312 | tf_op jit(solution)/shard_map/ppermute | solution.py:22
  36.6 8.5 %copy-start.7 = (s32[64]{0:T(128)S(1)}, s32[64]{0:T(128)}, u32[]{:S(2)}) copy-start(s32[64]{0:T(128)} %param.11) | copy-start | bytes 772
  36.7 8.5 %copy-start.4 = (s32[64,4]{0,1:T(4,128)S(1)}, s32[64,4]{0,1:T(4,128)}, u32[]{:S(2)}) copy-start(s32[64,4]{0,1:T(4,128)} %param.10) | copy-start | bytes 3076
  36.7 8.6 %copy-start = (bf16[64,8192]{1,0:T(8,128)(2,1)S(1)}, bf16[64,8192]{1,0:T(8,128)(2,1)}, u32[]{:S(2)}) copy-start(bf16[64,8192]{1,0:T(8,128)(2,1)} %param.7) | copy-start | bytes 3145732
  36.7 25.4 %all-to-all-start = ((bf16[32,2,8192]{2,1,0:T(2,128)(2,1)}), bf16[32,2,8192]{2,1,0:T(2,128)(2,1)S(1)}, u32[]{:S(2)}, u32[]{:S(2)}) async-start(bf16[32,2,8192]{2,1,0:T(2,128)(2,1)} %reshape.306), calls=%async_computation | async-start | bytes 2097152 | tf_op jit(solution)/shard_map/all_to_all | solution.py:34
  45.1 83.0 %all-gather.2.cloned.1.call-start = ((), (), s32[]{:S(2)}) async-start(), calls=%async_computation.3 | async-start | bytes 5242880 | tf_op jit(solution)/shard_map/all_gather | solution.py:54
  82.4 4.8 %slice-start = ((s8[8388608]{0:T(1024)(128)(4,1)}), s8[4194304]{0:T(1024)(128)(4,1)S(1)}, s32[]{:S(2)}) async-start(s8[8388608]{0:T(1024)(128)(4,1)} %bitcast.219), calls=%async_computation.4 | async-start | bytes 8388608
  86.3 3.1 %slice-start.1 = ((s8[8388608]{0:T(1024)(128)(4,1)}), s8[4194304]{0:T(1024)(128)(4,1)S(1)}, s32[]{:S(2)}) async-start(s8[8388608]{0:T(1024)(128)(4,1)} %bitcast.219), calls=%async_computation.5 | async-start | bytes 8388608
  86.9 15.1 %copy-start.1 = (bf16[8,64,8,128]{3,2,1,0:T(8,128)(2,1)}, bf16[8,64,8,128]{3,2,1,0:T(8,128)(2,1)S(1)}, u32[]{:S(2)}) copy-start(bf16[8,64,8,128]{3,2,1,0:T(8,128)(2,1)S(1)} %get-tuple-element.8) | copy-start | bytes 3145732
  87.2 21.1 %copy-start.2 = (bf16[8,64,8,128]{3,2,1,0:T(8,128)(2,1)}, bf16[8,64,8,128]{3,2,1,0:T(8,128)(2,1)S(1)}, u32[]{:S(2)}) copy-start(bf16[8,64,8,128]{3,2,1,0:T(8,128)(2,1)S(1)} %get-tuple-element.6) | copy-start | bytes 3145732
  112.4 15.7 %copy-start.6 = (bf16[16,64,4,64]{3,2,1,0:T(4,128)(2,1)S(1)}, bf16[16,64,4,64]{3,2,1,0:T(4,128)(2,1)}, u32[]{:S(2)}) copy-start(bf16[16,64,4,64]{3,2,1,0:T(4,128)(2,1)} %param.8) | copy-start | bytes 1572868
  132.6 17.8 %all-to-all-start.1 = ((bf16[16,4,64,128]{3,2,1,0:T(8,128)(2,1)}), bf16[16,4,64,128]{3,2,1,0:T(8,128)(2,1)S(1)}, u32[]{:S(2)}, u32[]{:S(2)}) async-start(bf16[16,4,64,128]{3,2,1,0:T(8,128)(2,1)} %copy.136), calls=%async_computation.1 | async-start | bytes 2097152 | tf_op jit(solution)/shard_map/all_to_all | solution.py:59
  152.2 25.7 %all-to-all-start.2 = ((bf16[4,16,64,128]{3,1,0,2:T(8,128)(2,1)}), bf16[4,16,64,128]{3,1,0,2:T(8,128)(2,1)}, u32[]{:S(2)}, u32[]{:S(2)}) async-start(bf16[4,16,64,128]{3,1,0,2:T(8,128)(2,1)} %copy.138), calls=%async_computation.2 | async-start | bytes 2097152 | tf_op jit(solution)/shard_map/all_to_all | solution.py:58
  182.2 2.7 %copy-start.3 = (f32[8192]{0:T(1024)S(1)}, f32[8192]{0:T(1024)}, u32[]{:S(2)}) copy-start(f32[8192]{0:T(1024)} %param.13) | copy-start | bytes 98308
  182.2 2.7 %copy-start.5 = (f32[64]{0:T(128)S(1)}, f32[64]{0:T(128)}, u32[]{:S(2)}) copy-start(f32[64]{0:T(128)} %param.12) | copy-start | bytes 772
Sparse Core Ops, SparseCore 0:
  82.5 45.5 all-gather.1
where the time goes:
time: 196 us; the launch traced here: 195 us
  matrix products  70.3 us (36%)
  local copies, waits for them, and re-layouts  56.1 us (29%)
  starting transfers between devices  27.8 us (14%)
  waiting for transfers between devices  23.5 us (12%)
  between operations  13.7 us (7%)
  other arithmetic  3.39 us (2%)
    dot_general x20, matrix products, local(): jnp.einsum('rcp,cpq->rcq', window, masked, preferred_element_type=jnp.flo...  66.9 us
    unnamed x25, local copies, waits for them, and re-layouts  21.7 us
    all_gather x1, waiting for transfers between devices, local(): all_rows = lax.all_gather(cycle_input, 'occ', axis=0, tiled=True)  13.6 us
    all_to_all x1, local copies, waits for them, and re-layouts, local(): lax.all_to_all(four_dim, 'vir', split_axis=3, concat_axis=2, tiled=True)  12.8 us
    reshape x2, local copies, waits for them, and re-layouts, local(): four_dim = amplitudes.reshape(outer_occ, NJ, NB_DEV, NA)  11.3 us
    all_to_all x1, starting transfers between devices, local(): lax.all_to_all(lax.all_to_all(cycle_part, 'occ', split_axis=0, concat_axi...  8.78 us
    all_to_all x1, starting transfers between devices, local(): lax.all_to_all(four_dim, 'vir', split_axis=3, concat_axis=2, tiled=True)  8.45 us
    all_to_all x1, waiting for transfers between devices, local(): lax.all_to_all(four_dim, 'vir', split_axis=3, concat_axis=2, tiled=True)  5.68 us
  transfers between devices with their start and end apart: 6, of which 4 were waited for; matrix products, arithmetic and copies ran while one was open for 57% of the time, Pallas kernels for 0%

commit v1 on v0

v1 whole, which is shorter than its diff:
```python
import jax
import jax.numpy as jnp
from jax import lax
from jax.experimental import pallas as pl
from jax.experimental.pallas import tpu as pltpu
from jax.sharding import PartitionSpec as P

TILE = 128
NV = 32
NO = 4
TILES = 64
MESH = pl.DeviceIdType.MESH
F32 = jnp.float32
BF16 = jnp.bfloat16


def lanes(tile):
    return pl.ds(pl.multiple_of(tile * TILE, TILE), TILE)


def kernel(
    rows_ref, count_ref, amp_ref, w_ref, tiles_ref, gap_ref, energy_ref, out_ref,
    near, tiles, spread, spread_wide, w_all, w_rows, back, landed, base, inverse,
    near_sem, tiles_sem, own_sem, w_own_sem, back_own_sem,
    halo_send, halo_recv, spread_send, spread_recv,
    w_send, w_recv, pass_send, pass_recv, back_send, back_recv,
):
    x = lax.axis_index("occ")
    v = lax.axis_index("vir")
    core = v % 2
    twin = v + 1 - 2 * core

    def load_tile(t):
        return pltpu.make_async_copy(amp_ref.at[:, lanes(t)], near.at[t + 2], near_sem.at[t])

    def load_ladder(q):
        return pltpu.make_async_copy(
            tiles_ref.at[pl.ds(q * 16, 16)], tiles.at[pl.ds(q * 16, 16)], tiles_sem.at[q]
        )

    def own_block(part):
        return pltpu.make_async_copy(
            amp_ref.at[:, lanes(part * NV + v)], spread.at[2 * v + part], own_sem.at[part]
        )

    own_w = pltpu.make_async_copy(w_ref, w_all.at[x], w_own_sem)

    @pl.loop(0, TILES)
    def _(t):
        load_tile(t).start()

    for q in range(4):
        load_ladder(q).start()
    own_w.start()
    for part in range(2):
        own_block(part).start()

    barrier = pltpu.get_barrier_semaphore()

    @pl.loop(1, NV)
    def _(d):
        pl.semaphore_signal(barrier, inc=1, device_id=(x, (v + d) % NV), device_id_type=MESH)

    for d in range(1, NO):
        pl.semaphore_signal(barrier, inc=1, device_id=((x + d) % NO, v), device_id_type=MESH)
    pl.semaphore_wait(barrier, NV - 1 + NO - 1)

    def halo(index):
        side, part = index // 2, index % 2
        tile = TILES - 2 + part if side == 0 else part
        slot = part if side == 0 else TILES + 2 + part
        peer = (v + 1) % NV if side == 0 else (v + NV - 1) % NV
        return pltpu.make_async_remote_copy(
            src_ref=amp_ref.at[:, tile * TILE : (tile + 1) * TILE],
            dst_ref=near.at[slot],
            send_sem=halo_send.at[index],
            recv_sem=halo_recv.at[index],
            device_id=(x, peer),
            device_id_type=MESH,
        )

    half = pl.ds(pl.multiple_of(core * 128, 128), 128)
    other_half = pl.ds(pl.multiple_of(128 - core * 128, 128), 128)

    def w_out(d, owner):
        return pltpu.make_async_remote_copy(
            src_ref=w_ref.at[half],
            dst_ref=w_all.at[owner, half],
            send_sem=w_send.at[d],
            recv_sem=w_recv.at[d],
            device_id=((x + d) % NO, v),
            device_id_type=MESH,
        )

    def w_pass(d, rows):
        owner = (x + NO - d) % NO
        return pltpu.make_async_remote_copy(
            src_ref=w_all.at[owner, rows],
            dst_ref=w_all.at[owner, rows],
            send_sem=pass_send.at[d],
            recv_sem=pass_recv.at[d],
            device_id=(x, twin),
            device_id_type=MESH,
        )

    def spread_out(d, part, source):
        target = (v + d) % NV
        return pltpu.make_async_remote_copy(
            src_ref=amp_ref.at[:, lanes(part * NV + target)],
            dst_ref=spread.at[2 * source + part],
            send_sem=spread_send.at[d, part],
            recv_sem=spread_recv.at[d, part],
            device_id=(x, target),
            device_id_type=MESH,
        )

    for index in range(4):
        halo(index).start()
    for d in (2, 1, 3):
        w_out(d, x).start()

    @pl.loop(1, NV)
    def _(d):
        for part in range(2):
            spread_out(d, part, v).start()

    near[TILES + 4] = jnp.zeros((64, TILE), BF16)
    row = lax.broadcasted_iota(jnp.int32, (64, 64), 0)
    column = lax.broadcasted_iota(jnp.int32, (64, 64), 1)
    gap = jnp.sum(jnp.where(row == column, gap_ref[...], 0.0), axis=1, keepdims=True)

    @pl.loop(0, TILES)
    def _(t):
        load_tile(t).wait()

    for index in range(4):
        halo(index).wait_recv()

    def ladder_tile(c):
        count = count_ref[c]
        picked = []
        for k in range(4):
            place = jnp.clip(rows_ref[k, c] - v * TILES + 2, 0, TILES + 3)
            if k >= 2:
                place = jnp.where(k < count, place, TILES + 4)
            picked.append(near[place])
        term = jnp.dot(jnp.concatenate(picked, axis=1), tiles[c], preferred_element_type=F32)
        scale = 1.0 / (gap + energy_ref[pl.ds(c, 1), :])
        inverse[c] = scale
        base[c] = near[c + 2].astype(F32) + term * scale

    for q in range(4):
        load_ladder(q).wait()

        @pl.loop(0, 4)
        def _(t):
            for step in range(4):
                ladder_tile(q * 16 + t * 4 + step)

    own_w.wait()
    for d in (1, 3, 2):
        w_out(d, (x + NO - d) % NO).wait_recv()
        w_pass(d, half).start()
    for d in (1, 3, 2):
        w_pass(d, other_half).wait_recv()

    r = lax.broadcasted_iota(jnp.int32, (256, 256), 0)
    c = lax.broadcasted_iota(jnp.int32, (256, 256), 1)
    source = ((r // 4) % 4) * 64 + (r // 16) * 4 + r % 4
    order = jnp.where(c == source, 1.0, 0.0).astype(BF16)
    for q in range(4):
        piece = jnp.concatenate([w_all[g, q * 64 : (q + 1) * 64, :] for g in range(NO)], axis=0)
        w_rows[q] = jnp.dot(order, piece, preferred_element_type=F32).astype(BF16)

    for part in range(2):
        own_block(part).wait()

    @pl.loop(1, NV)
    def _(d):
        for part in range(2):
            spread_out(d, part, (v + NV - d) % NV).wait_recv()

    for i in range(NO):
        spread_wide[:, i * TILE : (i + 1) * TILE] = spread[:, i * 16 : (i + 1) * 16, :].reshape(
            1024, TILE
        )

    group, member = v // 8, v % 8

    def back_out(s, e, origin):
        target = ((group + s) % 4) * 8 + (member + e) % 8
        return pltpu.make_async_remote_copy(
            src_ref=back.at[target],
            dst_ref=landed.at[origin],
            send_sem=back_send.at[s * 8 + e],
            recv_sem=back_recv.at[s * 8 + e],
            device_id=(x, target),
            device_id_type=MESH,
        )

    own_back = pltpu.make_async_copy(back.at[v], landed.at[v], back_own_sem)

    for s in range(4):
        q = (group + s) % 4
        product = jnp.dot(w_rows[q], spread_wide[...], preferred_element_type=F32).astype(BF16)
        for i in range(NO):
            back[pl.ds(q * 8, 8), :, i * 16 : (i + 1) * 16, :] = product[
                :, i * TILE : (i + 1) * TILE
            ].reshape(8, 2, 16, TILE)
        if s == 0:
            own_back.start()

        @pl.loop(1 if s == 0 else 0, 8)
        def _(e):
            back_out(s, e, v).start()

    def combine(origin):
        for part in range(2):
            tile = part * NV + origin
            value = base[tile] + landed[origin, part].astype(F32) * inverse[tile]
            out_ref[:, lanes(tile)] = value.astype(BF16)

    own_back.wait()
    combine(v)
    for s in range(4):

        @pl.loop(1 if s == 0 else 0, 8)
        def _(e):
            origin = ((group + 4 - s) % 4) * 8 + (member + 8 - e) % 8
            back_out(s, e, origin).wait_recv()
            combine(origin)

    for index in range(4):
        halo(index).wait_send()
    for d in range(1, NO):
        w_out(d, x).wait_send()
        w_pass(d, half).wait_send()

    @pl.loop(1, NV)
    def _(d):
        for part in range(2):
            spread_out(d, part, v).wait_send()

    for s in range(4):

        @pl.loop(1 if s == 0 else 0, 8)
        def _(e):
            back_out(s, e, v).wait_send()


def local(
    amplitudes, cycle_integrals, ladder_tiles, ladder_rows, ladder_count, row_gap, column_energy
):
    w_shard = jnp.transpose(cycle_integrals, (3, 2, 1, 0)).reshape(256, 1024)
    dma = pltpu.SemaphoreType.DMA
    any_space = pl.BlockSpec(memory_space=pl.ANY)
    smem = pl.BlockSpec(memory_space=pltpu.SMEM)
    vmem = pl.BlockSpec(memory_space=pltpu.VMEM)
    return pl.pallas_call(
        kernel,
        out_shape=jax.ShapeDtypeStruct((64, 8192), BF16),
        in_specs=[smem, smem, any_space, any_space, any_space, vmem, vmem],
        out_specs=vmem,
        scratch_shapes=[
            pltpu.VMEM((TILES + 5, 64, TILE), BF16),
            pltpu.VMEM((TILES, 512, TILE), BF16),
            pltpu.VMEM((64, 64, TILE), BF16),
            pltpu.VMEM((1024, 512), BF16),
            pltpu.VMEM((NO, 256, 1024), BF16),
            pltpu.VMEM((4, 256, 1024), BF16),
            pltpu.VMEM((NV, 2, 64, TILE), BF16),
            pltpu.VMEM((NV, 2, 64, TILE), BF16),
            pltpu.VMEM((TILES, 64, TILE), F32),
            pltpu.VMEM((TILES, 64, TILE), F32),
            dma((TILES,)),
            dma((4,)),
            dma((2,)),
            dma,
            dma,
            dma((4,)),
            dma((4,)),
            dma((NV, 2)),
            dma((NV, 2)),
            dma((NO,)),
            dma((NO,)),
            dma((NO,)),
            dma((NO,)),
            dma((NV,)),
            dma((NV,)),
        ],
        compiler_params=pltpu.CompilerParams(
            collective_id=0, has_side_effects=True, vmem_limit_bytes=60 * 2**20
        ),
    )(
        ladder_rows.T,
        ladder_count,
        amplitudes,
        w_shard,
        ladder_tiles.reshape(TILES, 512, TILE),
        row_gap.reshape(1, 64),
        column_energy.reshape(TILES, TILE),
    )


def solution(mesh):
    in_specs = (
        P("occ", "vir"),
        P(None, None, "occ", None),
        P("vir", None, None, None),
        P("vir", None),
        P("vir"),
        P("occ"),
        P("vir"),
    )
    return jax.shard_map(
        local, mesh=mesh, in_specs=in_specs, out_specs=P("occ", "vir"), check_vma=False
    )
```

time: 196 us -> 68.4 us (0.35)
  matrix products: 70.3 us -> 0 us
  Pallas kernels: 0 us -> 48.3 us
  local copies, waits for them, and re-layouts: 56.1 us -> 19.8 us
  starting transfers between devices: 27.8 us -> 0 us
  waiting for transfers between devices: 23.5 us -> 0 us
  between operations: 13.7 us -> 0.01 us
  other arithmetic: 3.39 us -> 0 us
    dot_general x21 -> x0, matrix products: 70.3 us -> none  [the longest x20 66.9 us: local(): jnp.einsum('rcp,cpq->rcq', window, masked, preferred_element_type=jnp.flo...]
    pallas_call x0 -> x1, Pallas kernels: none -> 48.3 us  [local(): pl.pallas_call(kernel, out_shape=jax.ShapeDtypeStruct((64, 8192), BF16),...]
    all_to_all x3 -> x0, starting transfers between devices: 21 us -> none  [the longest x1 8.78 us: local(): lax.all_to_all(lax.all_to_all(cycle_part, 'occ', split_axis=0, concat_axi...]
    unnamed x25 -> x1, local copies, waits for them, and re-layouts: 21.7 us -> 2.26 us
    all_to_all x4 -> x0, local copies, waits for them, and re-layouts: 15.9 us -> none  [the longest x1 12.8 us: local(): lax.all_to_all(four_dim, 'vir', split_axis=3, concat_axis=2, tiled=True)]
    all_gather x1 -> x0, waiting for transfers between devices: 13.6 us -> none  [local(): all_rows = lax.all_gather(cycle_input, 'occ', axis=0, tiled=True)]
    all_to_all x3 -> x0, waiting for transfers between devices: 9.84 us -> none  [the longest x1 5.68 us: local(): lax.all_to_all(four_dim, 'vir', split_axis=3, concat_axis=2, tiled=True)]
    transpose x0 -> x1, local copies, waits for them, and re-layouts: none -> 8.7 us  [local(): w_shard = jnp.transpose(cycle_integrals, (3, 2, 1, 0)).reshape(256, 1024)]
  transfers between devices with their start and end apart: 6 -> 0, of which waited for: 4 -> 0; matrix products, arithmetic and copies ran while one was open for 57% -> 0% of each run, Pallas kernels for 0% -> 0%
where the time goes in v1:
time: 68.4 us; the launch traced here: 68.2 us
  Pallas kernels  48.3 us (71%)
  local copies, waits for them, and re-layouts  19.8 us (29%)
    pallas_call x1, Pallas kernels, local(): pl.pallas_call(kernel, out_shape=jax.ShapeDtypeStruct((64, 8192), BF16),...  48.3 us
    reshape x1, local copies, waits for them, and re-layouts, local(): w_shard = jnp.transpose(cycle_integrals, (3, 2, 1, 0)).reshape(256, 1024)  8.83 us
    transpose x1, local copies, waits for them, and re-layouts, local(): w_shard = jnp.transpose(cycle_integrals, (3, 2, 1, 0)).reshape(256, 1024)  8.7 us
    unnamed x1, local copies, waits for them, and re-layouts  2.26 us

profile of v1, /device:TPU:1, one launch (start us, length us, event | category | flops | bytes accessed | tf_op | source)
XLA Modules:
  0.0 68.2 jit_solution(13803860409618085302)
XLA Ops:
  0.0 8.7 %copy.9 = bf16[64,4,64,16]{3,2,1,0:T(8,128)(2,1)} copy(bf16[64,4,64,16]{0,1,2,3:T(4,128)(2,1)} %bitcast.8) | data formatting | bytes 1048576 | tf_op jit(solution)/shard_map/transpose | solution.py:254
  8.7 8.8 %reshape.12.w_ref = bf16[256,1024]{1,0:T(8,128)(2,1)} reshape(bf16[64,4,64,16]{3,2,1,0:T(8,128)(2,1)} %copy.9) | data formatting | bytes 1048576 | tf_op jit(solution)/shard_map/reshape | solution.py:254
  17.5 48.3 %shard_map.73 = bf16[64,8192]{1,0:T(8,128)(2,1)} custom-call(s32[4,64]{1,0:T(4,128)} %bitcast.10, s32[64]{0:T(128)} %count_ref.1, bf16[64,8192]{1,0:T(8,128)(2,1)} %amp_ref.1, bf16[256,1024]{1,0:T(8,128)(2,1)} %reshape.12.w_ref, bf16[64,512,128]{2,1,0:T(8,128)(2,1)} %bitcast.7, f32[1,64]{1,0:T(1,128)} %bitcast.11, f32[64,128]{1,0:T(8,128)} %bitcast.9), custom_call_target="tpu_custom_call" | custom-call | tf_op jit(solution)/shard_map/pallas_call | solution.py:259
  65.9 2.3 %copy.11 = bf16[64,8192]{1,0:T(8,128)(2,1)} copy(bf16[64,8192]{1,0:T(8,128)(2,1)} %shard_map.73) | data formatting | bytes 2097152
